TPU v7x, 512 devices: a whole 4x8x8 slice. The times are simulated.
512 devices in a mesh: head: 32 (over y, z_lo), seq: 8 (over x, core), batch: 2 (over z_hi).
Axes of the slice: x: 4, y: 8, z: 8 (z_hi: 2, z_lo: 4; z = z_hi * 4 + z_lo), core: 2. Of those that a mesh axis runs over, the one named last changes fastest.
Arguments:
- teacher_qkv: bfloat16 [1, 128, 512, 8192], P(None, ('seq', 'batch'), None, 'head'), may hold values from -24 to 24
- student_qkv: bfloat16 [1, 128, 512, 4096], P(None, ('seq', 'batch'), 'head'), may hold values from -24 to 24
Outputs:
- student_grads: bfloat16 [1, 128, 512, 4096], P(None, ('seq', 'batch'), 'head')
All inputs are finite; a program needn't handle non-finite values.
Results may differ from a plain program's by a relative error of at most 0.0045.
Values may be sent and summed in bfloat16 or wider, within the bound.
A program may use at most 64 MiB of HBM per device.

v0:
```python
import math

import jax
import jax.numpy as jnp
from jax import lax
from jax.sharding import PartitionSpec as P

TEACHER_WIDTH = 8192
STUDENT_WIDTH = 4096
RELATION_HEADS = 64


def split_up(shard, dim, length):
    before, after = (shard.shape[:dim], shard.shape[dim + 1 :])
    return jnp.moveaxis(shard.reshape(*before, length, -1, *after), dim, 0)


def cut_rows(length, count):
    unit = 8 if length >= 8 * count else 1
    return [length // unit * k // count * unit for k in range(1, count)]


def laid_out(pieces, dim):
    pieces = jnp.moveaxis(pieces, 0, dim)
    dims = pieces.shape
    return pieces.reshape(*dims[:dim], dims[dim] * dims[dim + 1], *dims[dim + 2 :])


def exchange_in_pieces(shard, axis, pieces, split_dim, concat_dim):
    blocks = split_up(shard, split_dim, lax.axis_size(axis))
    cut = max(range(1, max(2, blocks.ndim - 1)), key=lambda d: blocks.shape[d])
    gathered = []
    for section in jnp.split(blocks, cut_rows(blocks.shape[cut], pieces), axis=cut):
        if section.size:
            gathered.append(lax.all_to_all(section, axis, split_axis=0, concat_axis=0, tiled=True))
    return laid_out(jnp.concatenate(gathered, axis=cut), concat_dim)


def softmax_rows(scores):
    row_peak = jnp.max(scores, axis=1, keepdims=True)
    weights = jnp.exp(scores - row_peak)
    return weights / jnp.sum(weights, axis=1, keepdims=True)


def item_gradient(teacher_rows, student_rows):
    teacher_width = TEACHER_WIDTH // RELATION_HEADS
    student_width = STUDENT_WIDTH // RELATION_HEADS
    teacher_factor = 1.0 / math.sqrt(teacher_width)
    student_factor = 1.0 / math.sqrt(student_width)
    head_count = teacher_rows.shape[1] // teacher_width
    head_parts = []
    for head in range(head_count):
        teacher_part = teacher_rows[:, head * teacher_width : (head + 1) * teacher_width]
        student_part = student_rows[:, head * student_width : (head + 1) * student_width]
        teacher_scores = (
            lax.dot_general(
                teacher_part,
                teacher_part,
                (((1,), (1,)), ((), ())),
                preferred_element_type=jnp.float32,
            )
            * teacher_factor
        )
        student_scores = (
            lax.dot_general(
                student_part,
                student_part,
                (((1,), (1,)), ((), ())),
                preferred_element_type=jnp.float32,
            )
            * student_factor
        )
        difference = (softmax_rows(student_scores) - softmax_rows(teacher_scores)).astype(
            jnp.bfloat16
        )
        query_side = jnp.dot(difference, student_part, preferred_element_type=jnp.float32)
        key_side = lax.dot_general(
            difference, student_part, (((0,), (0,)), ((), ())), preferred_element_type=jnp.float32
        )
        head_parts.append((query_side + key_side) * student_factor)
    return jnp.concatenate(head_parts, axis=1).astype(jnp.bfloat16)


def body(teacher_qkv, student_qkv):
    kind_count = teacher_qkv.shape[0]
    regrouped = exchange_in_pieces(student_qkv, "head", 2, 3, 2)
    item_count = kind_count * teacher_qkv.shape[1]
    teacher_items = teacher_qkv.reshape(item_count, teacher_qkv.shape[2], teacher_qkv.shape[3])
    student_items = regrouped.reshape(item_count, regrouped.shape[2], regrouped.shape[3])

    def one_item(loop_state, operands):
        return (loop_state, item_gradient(operands[0], operands[1]))

    final_state, gradients = lax.scan(one_item, 0, (teacher_items, student_items))
    gradients = gradients.reshape(regrouped.shape)
    return lax.all_to_all(gradients, "head", split_axis=2, concat_axis=3, tiled=True)


def solution(mesh):
    in_specs = (P(None, ("seq", "batch"), None, "head"), P(None, ("seq", "batch"), "head", None))
    out_specs = P(None, ("seq", "batch"), "head", None)
    return jax.shard_map(body, mesh=mesh, in_specs=in_specs, out_specs=out_specs, check_vma=False)
```

profile of v0, /device:TPU:6, one launch (start us, length us, event | category | flops | bytes accessed | tf_op | source)
XLA Modules:
  0.0 129.8 jit_solution(7658493632089525632)
XLA Ops:
  0.0 1.4 %copy.22 = bf16[16,8,32,128]{3,2,1,0:T(8,128)(2,1)S(1)} copy(bf16[16,8,32,128]{3,1,2,0:T(8,128)(2,1)} %bitcast.51) | data formatting | bytes 2097152
  1.6 1.0 copy.13
  2.5 12.9 %all-to-all-start = ((bf16[32,1,8,8,128]{4,3,2,1,0:T(8,128)(2,1)}), bf16[32,1,8,8,128]{4,3,2,1,0:T(8,128)(2,1)S(1)}, u32[]{:S(2)}, u32[]{:S(2)}) async-start(bf16[32,1,8,8,128]{4,3,2,1,0:T(8,128)(2,1)} %copy.13), calls=%async_computation | async-start | bytes 1048576 | tf_op jit(solution)/shard_map/all_to_all | solution.py:35
  15.5 1.0 copy.14
  16.5 17.3 %all-to-all-done = bf16[32,1,8,8,128]{4,3,2,1,0:T(8,128)(2,1)S(1)} async-done(((bf16[32,1,8,8,128]{4,3,2,1,0:T(8,128)(2,1)}), bf16[32,1,8,8,128]{4,3,2,1,0:T(8,128)(2,1)S(1)}, u32[]{:S(2)}, u32[]{:S(2)}) %all-to-all-start) | async-done | bytes 524320 | tf_op jit(solution)/shard_map/all_to_all | solution.py:35
  33.8 3.9 %all-to-all-start.1 = ((bf16[32,1,8,8,128]{4,3,2,1,0:T(8,128)(2,1)}), bf16[32,1,8,8,128]{4,3,2,1,0:T(8,128)(2,1)S(1)}, u32[]{:S(2)}, u32[]{:S(2)}) async-start(bf16[32,1,8,8,128]{4,3,2,1,0:T(8,128)(2,1)} %copy.14), calls=%async_computation.1 | async-start | bytes 1048576 | tf_op jit(solution)/shard_map/all_to_all | solution.py:35
  37.7 18.3 %all-to-all-done.1 = bf16[32,1,8,8,128]{4,3,2,1,0:T(8,128)(2,1)S(1)} async-done(((bf16[32,1,8,8,128]{4,3,2,1,0:T(8,128)(2,1)}), bf16[32,1,8,8,128]{4,3,2,1,0:T(8,128)(2,1)S(1)}, u32[]{:S(2)}, u32[]{:S(2)}) %all-to-all-start.1) | async-done | bytes 524320 | tf_op jit(solution)/shard_map/all_to_all | solution.py:35
  56.5 39.2 %while.10 = (s32[]{:T(128)}, bf16[8,512,128]{1,2,0:T(8,128)(2,1)S(1)}, bf16[8,512,128]{2,1,0:T(8,128)(2,1)S(1)}, bf16[8,512,256]{2,1,0:T(8,128)(2,1)}, s32[]{:T(128)}) while((s32[]{:T(128)}, bf16[8,512,128]{1,2,0:T(8,128)(2,1)S(1)}, bf16[8,512,128]{2,1,0:T(8,128)(2,1)S(1)}, bf16[8,512,256]{2,1,0:T(8,128)(2,1)}, s32[]{:T(128)}) %tuple.41), condition=%wide.region_9.10_spmd, body=%wide.region_0.9_spmd.sunk | while | flops 343339008 | bytes 18522184 | solution.py:94
  56.8 1.0 dynamic-slice_bitcast_fusion.5
  58.4 0.4 subtract_convert_fusion.5
  59.3 0.4 fusion.55
  60.3 0.4 subtract_convert_fusion.4
  61.0 0.4 fusion.59
  61.7 1.0 dynamic-slice_bitcast_fusion.5
  63.3 0.4 subtract_convert_fusion.5
  64.2 0.4 fusion.55
  65.2 0.4 subtract_convert_fusion.4
  65.9 0.4 fusion.59
  66.6 1.0 dynamic-slice_bitcast_fusion.5
  68.2 0.4 subtract_convert_fusion.5
  69.1 0.4 fusion.55
  70.1 0.4 subtract_convert_fusion.4
  71.5 1.0 dynamic-slice_bitcast_fusion.5
  73.1 0.4 subtract_convert_fusion.5
  74.0 0.4 fusion.55
  75.0 0.4 subtract_convert_fusion.4
  75.7 0.4 fusion.59
  76.4 1.0 dynamic-slice_bitcast_fusion.5
  78.0 0.4 subtract_convert_fusion.5
  78.9 0.4 fusion.55
  79.9 0.4 subtract_convert_fusion.4
  80.6 0.4 fusion.59
  81.3 1.0 dynamic-slice_bitcast_fusion.5
  82.9 0.4 subtract_convert_fusion.5
  83.8 0.4 fusion.55
  84.8 0.4 subtract_convert_fusion.4
  86.2 1.0 dynamic-slice_bitcast_fusion.5
  87.8 0.4 subtract_convert_fusion.5
  88.7 0.4 fusion.55
  89.7 0.4 subtract_convert_fusion.4
  90.4 0.4 fusion.59
  91.1 1.0 dynamic-slice_bitcast_fusion.5
  92.7 0.4 subtract_convert_fusion.5
  93.6 0.4 fusion.55
  94.6 0.4 subtract_convert_fusion.4
  95.7 0.8 copy.17
  96.5 32.0 %all_to_all.28 = bf16[1,8,512,128]{3,1,0,2:T(8,128)(2,1)S(1)} all-to-all(bf16[1,8,512,128]{3,1,0,2:T(8,128)(2,1)S(1)} %bitcast.48), channel_id=1, replica_groups=mesh['head'=32,'seq'=8,'batch'=2] {'head'}, dimensions={2} | all-to-all | bytes 2097152 | tf_op jit(solution)/shard_map/all_to_all | solution.py:96
  128.6 1.2 copy.24
  (88 shorter events, 20.8 us)
Async XLA Ops:
  2.5 31.3 %all-to-all-start = ((bf16[32,1,8,8,128]{4,3,2,1,0:T(8,128)(2,1)}), bf16[32,1,8,8,128]{4,3,2,1,0:T(8,128)(2,1)S(1)}, u32[]{:S(2)}, u32[]{:S(2)}) async-start(bf16[32,1,8,8,128]{4,3,2,1,0:T(8,128)(2,1)} %copy.13), calls=%async_computation | async-start | bytes 1048576 | tf_op jit(solution)/shard_map/all_to_all | solution.py:35
  33.8 22.3 %all-to-all-start.1 = ((bf16[32,1,8,8,128]{4,3,2,1,0:T(8,128)(2,1)}), bf16[32,1,8,8,128]{4,3,2,1,0:T(8,128)(2,1)S(1)}, u32[]{:S(2)}, u32[]{:S(2)}) async-start(bf16[32,1,8,8,128]{4,3,2,1,0:T(8,128)(2,1)} %copy.14), calls=%async_computation.1 | async-start | bytes 1048576 | tf_op jit(solution)/shard_map/all_to_all | solution.py:35
where the time goes:
time: 131 us; the launch traced here: 130 us
  waiting for transfers between devices  35.7 us (27%)
  blocking collectives  32 us (24%)
  matrix products  20.1 us (15%)
  starting transfers between devices  16.8 us (13%)
  local copies, waits for them, and re-layouts  13.7 us (10%)
  other arithmetic  10.8 us (8%)
    all_to_all x2, waiting for transfers between devices, exchange_in_pieces(): lax.all_to_all(section, axis, split_axis=0, concat_axis=0, tiled=True)  35.7 us
    all_to_all x1, blocking collectives, body(): lax.all_to_all(gradients, 'head', split_axis=2, concat_axis=3, tiled=True)  32 us
    all_to_all x2, starting transfers between devices, exchange_in_pieces(): lax.all_to_all(section, axis, split_axis=0, concat_axis=0, tiled=True)  16.8 us
    squeeze x16, local copies, waits for them, and re-layouts, body(): lax.scan(one_item, 0, (teacher_items, student_items))  7.91 us
    convert_element_type x16, other arithmetic, item_gradient(): (softmax_rows(student_scores) - softmax_rows(teacher_scores)).astype(jnp....  5.74 us
    dot_general x16, matrix products, item_gradient(): lax.dot_general(student_part, student_part, (((1,), (1,)), ((), ())), pre...  5.58 us
    dot_general x16, matrix products, item_gradient(): lax.dot_general(difference, student_part, (((0,), (0,)), ((), ())), prefe...  5.18 us
    dot_general x16, matrix products, item_gradient(): lax.dot_general(teacher_part, teacher_part, (((1,), (1,)), ((), ())), pre...  4.93 us
  transfers between devices with their start and end apart: 2, of which 2 were waited for; matrix products, arithmetic and copies ran while one was open for 1% of the time, Pallas kernels for 0%

commit v1 on v0

v1 whole, which is shorter than its diff:
```python
import functools
import math

import jax
import jax.numpy as jnp
from jax import lax
from jax.experimental import pallas as pl
from jax.experimental.pallas import tpu as pltpu
from jax.sharding import PartitionSpec as P

RELATION_HEADS = 64
CHUNK = 2
STRIP = 256
LOG2E = 1.4426950408889634
F32, BF16 = jnp.float32, jnp.bfloat16
MESH = pl.DeviceIdType.MESH
NT = (((1,), (1,)), ((), ()))


def probs(rows, some, factor):
    scores = lax.dot_general(rows, some, NT, preferred_element_type=F32)
    peak = jnp.max(scores, axis=0, keepdims=True)
    weights = jnp.exp2((scores - peak) * factor)
    return weights * (1.0 / jnp.sum(weights, axis=0, keepdims=True))


def item_gradient(heads, teacher, student, grads, diff):
    length = teacher.shape[0]
    tw, sw = teacher.shape[1] // heads, student.shape[1] // heads
    x = student[...]
    lane = lax.broadcasted_iota(jnp.int32, x.shape, 1)
    x_t = x.T
    parts = []
    for head in range(heads):
        mine = (lane >= head * sw) & (lane < (head + 1) * sw)
        xh = jnp.where(mine, x, jnp.zeros_like(x))
        th = teacher[:, head * tw : (head + 1) * tw]
        for i in range(0, length, STRIP):
            student_probs = probs(x, xh[i : i + STRIP], LOG2E / math.sqrt(sw))
            teacher_probs = probs(th, th[i : i + STRIP], LOG2E / math.sqrt(tw))
            diff[:, i : i + STRIP] = (student_probs - teacher_probs).astype(BF16)
        xh_t = x_t[head * sw : (head + 1) * sw]
        d = diff[...]
        key_side = lax.dot_general(xh_t, d, NT, preferred_element_type=F32)
        query_side = jnp.dot(xh_t, d, preferred_element_type=F32)
        parts.append(query_side + key_side)
    grads_t = jnp.concatenate(parts, axis=0) * (1.0 / math.sqrt(sw))
    grads[...] = grads_t.T.astype(BF16)


def kernel(ny, nz, heads, teacher_hbm, student_hbm, out, teacher, staged, xs, grads, diff, sems, in_recv, t_sem):
    n = ny * nz
    me = lax.axis_index("head")
    y, z = me // nz, me % nz
    items, rows, _ = staged.shape
    width = xs.shape[2]
    load_sem, in_send, out_send, out_recv = (sems.at[i] for i in range(4))

    def peer(t):
        a, dz = t // nz, t % nz
        dy = (a % 2) * ((a + 1) // 2) + (1 - a % 2) * (ny - a // 2)
        return ((y + dy) % ny) * nz + (z + dz) % nz

    load = pltpu.make_async_copy(student_hbm, staged, load_sem)
    load.start()

    def load_teacher(b, _):
        pltpu.make_async_copy(teacher_hbm.at[b], teacher.at[b], t_sem.at[b]).start()
        return 0

    lax.fori_loop(0, items, load_teacher, 0)

    barrier = pltpu.get_barrier_semaphore()

    def greet(t, _):
        pl.semaphore_signal(barrier, inc=1, device_id={"head": peer(t)}, device_id_type=MESH)
        return 0

    lax.fori_loop(1, n, greet, 0)
    load.wait()
    pl.semaphore_wait(barrier, n - 1)

    my_rows = pl.ds(pl.multiple_of(me * rows, rows), rows)
    my_cols = pl.ds(pl.multiple_of(me * width, width), width)

    def send_in(c, _):
        batch = pl.ds(c * CHUNK, CHUNK)
        pltpu.make_async_copy(
            staged.at[batch, :, my_cols], xs.at[batch, my_rows, :], in_recv.at[c]
        ).start()

        def to(t, _):
            p = peer(t)
            pltpu.make_async_remote_copy(
                src_ref=staged.at[batch, :, pl.ds(pl.multiple_of(p * width, width), width)],
                dst_ref=xs.at[batch, my_rows, :],
                send_sem=in_send,
                recv_sem=in_recv.at[c],
                device_id={"head": p},
                device_id_type=MESH,
            ).start()
            return 0

        lax.fori_loop(1, n, to, 0)
        return 0

    lax.fori_loop(0, items // CHUNK, send_in, 0)

    def work(c, _):
        batch = pl.ds(c * CHUNK, CHUNK)
        pltpu.make_async_copy(xs.at[batch], xs.at[batch], in_recv.at[c]).wait()
        for k in range(CHUNK):
            b = c * CHUNK + k
            pltpu.make_async_copy(teacher_hbm.at[b], teacher.at[b], t_sem.at[b]).wait()
            item_gradient(heads, teacher.at[b], xs.at[b], grads.at[b], diff)
        pltpu.make_async_copy(
            grads.at[batch, my_rows, :], out.at[batch, :, my_cols], out_recv
        ).start()

        def to(t, _):
            p = peer(t)
            pltpu.make_async_remote_copy(
                src_ref=grads.at[batch, pl.ds(pl.multiple_of(p * rows, rows), rows), :],
                dst_ref=out.at[batch, :, my_cols],
                send_sem=out_send,
                recv_sem=out_recv,
                device_id={"head": p},
                device_id_type=MESH,
            ).start()
            return 0

        lax.fori_loop(1, n, to, 0)
        return 0

    lax.fori_loop(0, items // CHUNK, work, 0)

    some = pl.ds(0, (n - 1) * rows)
    pltpu.make_async_copy(xs.at[:, some, :], xs.at[:, some, :], in_send).wait()
    pltpu.make_async_copy(grads.at[:, some, :], grads.at[:, some, :], out_send).wait()
    pltpu.make_async_copy(out, out, out_recv).wait()


def solution(mesh):
    n = mesh.shape["head"]
    nz = 4
    heads = RELATION_HEADS // n

    def body(teacher_qkv, student_qkv):
        _, items, length, teacher_width = teacher_qkv.shape
        _, _, rows, student_width = student_qkv.shape
        width = student_width // n
        result = pl.pallas_call(
            functools.partial(kernel, n // nz, nz, heads),
            out_shape=jax.ShapeDtypeStruct((items, rows, student_width), BF16),
            in_specs=[pl.BlockSpec(memory_space=pltpu.HBM)] * 2,
            out_specs=pl.BlockSpec(memory_space=pl.ANY),
            scratch_shapes=[
                pltpu.VMEM((items, length, teacher_width), BF16),
                pltpu.VMEM((items, rows, student_width), BF16),
                pltpu.VMEM((items, length, width), BF16),
                pltpu.VMEM((items, length, width), BF16),
                pltpu.VMEM((length, length), BF16),
                pltpu.SemaphoreType.DMA((4,)),
                pltpu.SemaphoreType.DMA((items // CHUNK,)),
                pltpu.SemaphoreType.DMA((items,)),
            ],
            compiler_params=pltpu.CompilerParams(
                collective_id=0, has_side_effects=True, vmem_limit_bytes=24 * 2**20
            ),
            name="relation_grads",
        )(teacher_qkv[0], student_qkv[0])
        return result[None]

    in_specs = (P(None, ("seq", "batch"), None, "head"), P(None, ("seq", "batch"), "head", None))
    out_specs = P(None, ("seq", "batch"), "head", None)
    return jax.shard_map(body, mesh=mesh, in_specs=in_specs, out_specs=out_specs, check_vma=False)
```

time: 131 us -> 64.3 us (0.49)
  Pallas kernels: 0 us -> 59.2 us
  waiting for transfers between devices: 35.7 us -> 0 us
  blocking collectives: 32 us -> 0 us
  matrix products: 20.1 us -> 0 us
  starting transfers between devices: 16.8 us -> 0 us
  other arithmetic: 10.8 us -> 0 us
  local copies, waits for them, and re-layouts: 13.7 us -> 3.79 us
    pallas_call x0 -> x1, Pallas kernels: none -> 59.2 us  [body(): pl.pallas_call(functools.partial(kernel, n // nz, nz, heads), out_shape=j...]
    all_to_all x2 -> x0, waiting for transfers between devices: 35.7 us -> none  [exchange_in_pieces(): lax.all_to_all(section, axis, split_axis=0, concat_axis=0, tiled=True)]
    all_to_all x1 -> x0, blocking collectives: 32 us -> none  [body(): lax.all_to_all(gradients, 'head', split_axis=2, concat_axis=3, tiled=True)]
    dot_general x64 -> x0, matrix products: 20.1 us -> none  [the longest x16 5.58 us: item_gradient(): lax.dot_general(student_part, student_part, (((1,), (1,)), ((), ())), pre...]
    all_to_all x2 -> x0, starting transfers between devices: 16.8 us -> none  [exchange_in_pieces(): lax.all_to_all(section, axis, split_axis=0, concat_axis=0, tiled=True)]
    squeeze x16 -> x0, local copies, waits for them, and re-layouts: 7.91 us -> none  [body(): lax.scan(one_item, 0, (teacher_items, student_items))]
    convert_element_type x16 -> x0, other arithmetic: 5.74 us -> none  [item_gradient(): (softmax_rows(student_scores) - softmax_rows(teacher_scores)).astype(jnp....]
    reduce_sum x16 -> x0, other arithmetic: 4.82 us -> none  [softmax_rows(): return weights / jnp.sum(weights, axis=1, keepdims=True)]
  transfers between devices with their start and end apart: 2 -> 0, of which waited for: 2 -> 0; matrix products, arithmetic and copies ran while one was open for 1% -> 0% of each run, Pallas kernels for 0% -> 0%
where the time goes in v1:
time: 64.3 us; the launch traced here: 63 us
  Pallas kernels  59.2 us (92%)
  local copies, waits for them, and re-layouts  3.79 us (6%)
    pallas_call x1, Pallas kernels, body(): pl.pallas_call(functools.partial(kernel, n // nz, nz, heads), out_shape=j...  59.2 us
    unnamed x5, local copies, waits for them, and re-layouts  3.79 us

profile of v1, /device:TPU:6, one launch (start us, length us, event | category | flops | bytes accessed | tf_op | source)
XLA Modules:
  0.0 63.0 jit_solution(16722674540594794754)
XLA Ops:
  0.0 0.0 copy-start
  0.0 1.6 %copy-done = bf16[1,8,512,256]{3,2,1,0:T(8,128)(2,1)S(1)} copy-done((bf16[1,8,512,256]{3,2,1,0:T(8,128)(2,1)S(1)}, bf16[1,8,512,256]{3,2,1,0:T(8,128)(2,1)}, u32[]{:S(2)}) %copy-start) | copy-done | bytes 2097176
  1.6 0.0 copy-start.1
  1.6 1.2 %copy-done.1 = bf16[1,8,16,4096]{3,2,1,0:T(8,128)(2,1)S(1)} copy-done((bf16[1,8,16,4096]{3,2,1,0:T(8,128)(2,1)S(1)}, bf16[1,8,16,4096]{3,2,1,0:T(8,128)(2,1)}, u32[]{:S(2)}) %copy-start.1) | copy-done | bytes 1048600
  2.8 59.2 %relation_grads.1 = bf16[8,16,4096]{2,1,0:T(8,128)(2,1)S(1)} custom-call(bf16[8,512,256]{2,1,0:T(8,128)(2,1)S(1)} %bitcast.4, bf16[8,16,4096]{2,1,0:T(8,128)(2,1)S(1)} %bitcast.5), custom_call_target="tpu_custom_call" | custom-call | tf_op jit(solution)/shard_map/relation_grads/pallas_call | solution.py:152
  62.1 1.0 %copy.4 = bf16[1,8,16,4096]{3,2,1,0:T(8,128)(2,1)} copy(bf16[1,8,16,4096]{3,2,1,0:T(8,128)(2,1)S(1)} %bitcast.3) | data formatting | bytes 2097152
Async XLA Ops:
  0.0 1.6 %copy-start = (bf16[1,8,512,256]{3,2,1,0:T(8,128)(2,1)S(1)}, bf16[1,8,512,256]{3,2,1,0:T(8,128)(2,1)}, u32[]{:S(2)}) copy-start(bf16[1,8,512,256]{3,2,1,0:T(8,128)(2,1)} %param.2) | copy-start | bytes 6291460
  1.6 1.2 %copy-start.1 = (bf16[1,8,16,4096]{3,2,1,0:T(8,128)(2,1)S(1)}, bf16[1,8,16,4096]{3,2,1,0:T(8,128)(2,1)}, u32[]{:S(2)}) copy-start(bf16[1,8,16,4096]{3,2,1,0:T(8,128)(2,1)} %param.3) | copy-start | bytes 3145732

commit v2 on v1

--- a/solution.py
+++ b/solution.py
@@ -11,6 +11,7 @@
 RELATION_HEADS = 64
 CHUNK = 2
 STRIP = 256
+EARLY = 3
 LOG2E = 1.4426950408889634
 F32, BF16 = jnp.float32, jnp.bfloat16
 MESH = pl.DeviceIdType.MESH
@@ -48,7 +49,7 @@
     grads[...] = grads_t.T.astype(BF16)
 
 
-def kernel(ny, nz, heads, teacher_hbm, student_hbm, out, teacher, staged, xs, grads, diff, sems, in_recv, t_sem):
+def kernel(ny, nz, heads, teacher_hbm, student_hbm, out, teacher, staged, xs, grads, diff, sems, in_recv, t_sem, level_sem):
     n = ny * nz
     me = lax.axis_index("head")
     y, z = me // nz, me % nz
@@ -70,41 +71,70 @@
 
     lax.fori_loop(0, items, load_teacher, 0)
 
-    barrier = pltpu.get_barrier_semaphore()
-
-    def greet(t, _):
-        pl.semaphore_signal(barrier, inc=1, device_id={"head": peer(t)}, device_id_type=MESH)
-        return 0
-
-    lax.fori_loop(1, n, greet, 0)
-    load.wait()
-    pl.semaphore_wait(barrier, n - 1)
+    def near(act):
+        for step in (1, ny - 1):
+            act((y + step) % ny, z)
+        pl.when(z > 0)(lambda: act(y, z - 1))
+        pl.when(z < nz - 1)(lambda: act(y, z + 1))
+
+    neighbours = 2 + (z > 0).astype(jnp.int32) + (z < nz - 1).astype(jnp.int32)
 
     my_rows = pl.ds(pl.multiple_of(me * rows, rows), rows)
     my_cols = pl.ds(pl.multiple_of(me * width, width), width)
 
-    def send_in(c, _):
+    def send_in(c, p):
+        batch = pl.ds(c * CHUNK, CHUNK)
+        pltpu.make_async_remote_copy(
+            src_ref=staged.at[batch, :, pl.ds(pl.multiple_of(p * width, width), width)],
+            dst_ref=xs.at[batch, my_rows, :],
+            send_sem=in_send,
+            recv_sem=in_recv.at[c],
+            device_id={"head": p},
+            device_id_type=MESH,
+        ).start()
+
+    def at_distance(c, lo, hi):
+        for dy in sorted(range(-((ny - 1) // 2), ny // 2 + 1), key=abs):
+            for dz in sorted(range(1 - nz, nz), key=abs):
+                if lo <= abs(dy) + abs(dz) <= hi:
+                    to = lambda dy=dy, dz=dz: send_in(c, (y + dy + ny) % ny * nz + z + dz)
+                    if dz:
+                        pl.when((z + dz >= 0) & (z + dz < nz))(to)
+                    else:
+                        to()
+
+    def all_chunks(lo, hi):
+        def one(c, _):
+            at_distance(c, lo, hi)
+            return 0
+
+        lax.fori_loop(0, items // CHUNK, one, 0)
+
+    barrier = pltpu.get_barrier_semaphore()
+    near(lambda yy, zz: pl.semaphore_signal(
+        barrier, inc=1, device_id={"head": yy * nz + zz}, device_id_type=MESH
+    ))
+    load.wait()
+
+    def own(c, _):
         batch = pl.ds(c * CHUNK, CHUNK)
         pltpu.make_async_copy(
             staged.at[batch, :, my_cols], xs.at[batch, my_rows, :], in_recv.at[c]
         ).start()
-
-        def to(t, _):
-            p = peer(t)
-            pltpu.make_async_remote_copy(
-                src_ref=staged.at[batch, :, pl.ds(pl.multiple_of(p * width, width), width)],
-                dst_ref=xs.at[batch, my_rows, :],
-                send_sem=in_send,
-                recv_sem=in_recv.at[c],
-                device_id={"head": p},
-                device_id_type=MESH,
-            ).start()
-            return 0
-
-        lax.fori_loop(1, n, to, 0)
         return 0
 
-    lax.fori_loop(0, items // CHUNK, send_in, 0)
+    lax.fori_loop(0, items // CHUNK, own, 0)
+    pl.semaphore_wait(barrier, neighbours)
+    farthest = ny // 2 + nz - 1
+    for level in range(1, farthest + 1):
+        if level > 1:
+            near(lambda yy, zz: pl.semaphore_signal(
+                level_sem.at[level - 2], inc=1, device_id={"head": yy * nz + zz}, device_id_type=MESH
+            ))
+            pl.semaphore_wait(level_sem.at[level - 2], neighbours)
+        if level <= EARLY:
+            all_chunks(level, level)
+    all_chunks(EARLY + 1, farthest)
 
     def work(c, _):
         batch = pl.ds(c * CHUNK, CHUNK)
@@ -151,9 +181,9 @@
         width = student_width // n
         result = pl.pallas_call(
             functools.partial(kernel, n // nz, nz, heads),
-            out_shape=jax.ShapeDtypeStruct((items, rows, student_width), BF16),
-            in_specs=[pl.BlockSpec(memory_space=pltpu.HBM)] * 2,
-            out_specs=pl.BlockSpec(memory_space=pl.ANY),
+            out_shape=pltpu.VMEM((items, rows, student_width), BF16),
+            in_specs=[pl.BlockSpec(memory_space=pl.ANY)] * 2,
+            out_specs=pl.BlockSpec(memory_space=pltpu.VMEM),
             scratch_shapes=[
                 pltpu.VMEM((items, length, teacher_width), BF16),
                 pltpu.VMEM((items, rows, student_width), BF16),
@@ -163,12 +193,13 @@
                 pltpu.SemaphoreType.DMA((4,)),
                 pltpu.SemaphoreType.DMA((items // CHUNK,)),
                 pltpu.SemaphoreType.DMA((items,)),
+                pltpu.SemaphoreType.REGULAR((n // nz // 2 + nz - 2,)),
             ],
             compiler_params=pltpu.CompilerParams(
-                collective_id=0, has_side_effects=True, vmem_limit_bytes=24 * 2**20
+                collective_id=0, has_side_effects=True, vmem_limit_bytes=40 * 2**20
             ),
             name="relation_grads",
-        )(teacher_qkv[0], student_qkv[0])
+        )(*(pltpu.with_memory_space_constraint(a[0], pltpu.HBM) for a in (teacher_qkv, student_qkv)))
         return result[None]
 
     in_specs = (P(None, ("seq", "batch"), None, "head"), P(None, ("seq", "batch"), "head", None))

time: 64.3 us -> 60.6 us (0.942); the launches traced: 63 us -> 60.2 us
  local copies, waits for them, and re-layouts: 3.79 us -> 0.97 us
    unnamed x5 -> x1, local copies, waits for them, and re-layouts: 3.79 us -> 0.97 us
where the time goes in v2:
time: 60.6 us; the launch traced here: 60.2 us
  Pallas kernels  59.3 us (98%)
  local copies, waits for them, and re-layouts  0.97 us (2%)
    pallas_call x1, Pallas kernels, body(): pl.pallas_call(functools.partial(kernel, n // nz, nz, heads), out_shape=p...  59.3 us

profile of v2, /device:TPU:6, one launch (start us, length us, event | category | flops | bytes accessed | tf_op | source)
XLA Modules:
  0.0 60.2 jit_solution(7064814769812787963)
XLA Ops:
  0.0 59.3 %relation_grads.1 = bf16[8,16,4096]{2,1,0:T(8,128)(2,1)S(1)} custom-call(bf16[8,512,256]{2,1,0:T(8,128)(2,1)} %bitcast.4, bf16[8,16,4096]{2,1,0:T(8,128)(2,1)} %bitcast.5), custom_call_target="tpu_custom_call" | custom-call | tf_op jit(solution)/shard_map/relation_grads/pallas_call | solution.py:182
  59.3 1.0 %copy.4 = bf16[1,8,16,4096]{3,2,1,0:T(8,128)(2,1)} copy(bf16[1,8,16,4096]{3,2,1,0:T(8,128)(2,1)S(1)} %bitcast.3) | data formatting | bytes 2097152

commit v3 on v2

--- a/solution.py
+++ b/solution.py
@@ -49,21 +49,13 @@
     grads[...] = grads_t.T.astype(BF16)
 
 
-def kernel(ny, nz, heads, teacher_hbm, student_hbm, out, teacher, staged, xs, grads, diff, sems, in_recv, t_sem, level_sem):
+def kernel(ny, nz, heads, teacher_hbm, student_hbm, out, teacher, xs, grads, diff, sems, in_recv, t_sem, level_sem):
     n = ny * nz
     me = lax.axis_index("head")
     y, z = me // nz, me % nz
-    items, rows, _ = staged.shape
+    items, rows, _ = student_hbm.shape
     width = xs.shape[2]
-    load_sem, in_send, out_send, out_recv = (sems.at[i] for i in range(4))
-
-    def peer(t):
-        a, dz = t // nz, t % nz
-        dy = (a % 2) * ((a + 1) // 2) + (1 - a % 2) * (ny - a // 2)
-        return ((y + dy) % ny) * nz + (z + dz) % nz
-
-    load = pltpu.make_async_copy(student_hbm, staged, load_sem)
-    load.start()
+    in_send, out_send, out_recv = (sems.at[i] for i in range(3))
 
     def load_teacher(b, _):
         pltpu.make_async_copy(teacher_hbm.at[b], teacher.at[b], t_sem.at[b]).start()
@@ -85,7 +77,7 @@
     def send_in(c, p):
         batch = pl.ds(c * CHUNK, CHUNK)
         pltpu.make_async_remote_copy(
-            src_ref=staged.at[batch, :, pl.ds(pl.multiple_of(p * width, width), width)],
+            src_ref=student_hbm.at[batch, :, pl.ds(pl.multiple_of(p * width, width), width)],
             dst_ref=xs.at[batch, my_rows, :],
             send_sem=in_send,
             recv_sem=in_recv.at[c],
@@ -93,11 +85,11 @@
             device_id_type=MESH,
         ).start()
 
-    def at_distance(c, lo, hi):
+    def peers(send, lo, hi):
         for dy in sorted(range(-((ny - 1) // 2), ny // 2 + 1), key=abs):
             for dz in sorted(range(1 - nz, nz), key=abs):
                 if lo <= abs(dy) + abs(dz) <= hi:
-                    to = lambda dy=dy, dz=dz: send_in(c, (y + dy + ny) % ny * nz + z + dz)
+                    to = lambda dy=dy, dz=dz: send((y + dy + ny) % ny * nz + z + dz)
                     if dz:
                         pl.when((z + dz >= 0) & (z + dz < nz))(to)
                     else:
@@ -105,7 +97,7 @@
 
     def all_chunks(lo, hi):
         def one(c, _):
-            at_distance(c, lo, hi)
+            peers(lambda p: send_in(c, p), lo, hi)
             return 0
 
         lax.fori_loop(0, items // CHUNK, one, 0)
@@ -114,12 +106,11 @@
     near(lambda yy, zz: pl.semaphore_signal(
         barrier, inc=1, device_id={"head": yy * nz + zz}, device_id_type=MESH
     ))
-    load.wait()
 
     def own(c, _):
         batch = pl.ds(c * CHUNK, CHUNK)
         pltpu.make_async_copy(
-            staged.at[batch, :, my_cols], xs.at[batch, my_rows, :], in_recv.at[c]
+            student_hbm.at[batch, :, my_cols], xs.at[batch, my_rows, :], in_recv.at[c]
         ).start()
         return 0
 
@@ -128,10 +119,11 @@
     farthest = ny // 2 + nz - 1
     for level in range(1, farthest + 1):
         if level > 1:
+            pl.semaphore_wait(level_sem.at[level - 2], neighbours)
+        if level < farthest:
             near(lambda yy, zz: pl.semaphore_signal(
-                level_sem.at[level - 2], inc=1, device_id={"head": yy * nz + zz}, device_id_type=MESH
+                level_sem.at[level - 1], inc=1, device_id={"head": yy * nz + zz}, device_id_type=MESH
             ))
-            pl.semaphore_wait(level_sem.at[level - 2], neighbours)
         if level <= EARLY:
             all_chunks(level, level)
     all_chunks(EARLY + 1, farthest)
@@ -147,8 +139,7 @@
             grads.at[batch, my_rows, :], out.at[batch, :, my_cols], out_recv
         ).start()
 
-        def to(t, _):
-            p = peer(t)
+        def send_out(p):
             pltpu.make_async_remote_copy(
                 src_ref=grads.at[batch, pl.ds(pl.multiple_of(p * rows, rows), rows), :],
                 dst_ref=out.at[batch, :, my_cols],
@@ -157,9 +148,15 @@
                 device_id={"head": p},
                 device_id_type=MESH,
             ).start()
-            return 0
-
-        lax.fori_loop(1, n, to, 0)
+
+        last = items // CHUNK - 1
+        pl.when(c < last)(lambda: peers(send_out, 1, farthest))
+
+        @pl.when(c == last)
+        def _():
+            for hops in range(farthest, 0, -1):
+                peers(send_out, hops, hops)
+
         return 0
 
     lax.fori_loop(0, items // CHUNK, work, 0)
@@ -186,11 +183,10 @@
             out_specs=pl.BlockSpec(memory_space=pltpu.VMEM),
             scratch_shapes=[
                 pltpu.VMEM((items, length, teacher_width), BF16),
-                pltpu.VMEM((items, rows, student_width), BF16),
                 pltpu.VMEM((items, length, width), BF16),
                 pltpu.VMEM((items, length, width), BF16),
                 pltpu.VMEM((length, length), BF16),
-                pltpu.SemaphoreType.DMA((4,)),
+                pltpu.SemaphoreType.DMA((3,)),
                 pltpu.SemaphoreType.DMA((items // CHUNK,)),
                 pltpu.SemaphoreType.DMA((items,)),
                 pltpu.SemaphoreType.REGULAR((n // nz // 2 + nz - 2,)),

time: 60.6 us -> 60 us (0.990)
  no operation moved by 1% of the time
where the time goes in v3:
time: 60 us; the launch traced here: 59.9 us
  Pallas kernels  58.9 us (98%)
  local copies, waits for them, and re-layouts  0.97 us (2%)
    pallas_call x1, Pallas kernels, body(): pl.pallas_call(functools.partial(kernel, n // nz, nz, heads), out_shape=p...  58.9 us

profile of v3, /device:TPU:6, one launch (start us, length us, event | category | flops | bytes accessed | tf_op | source)
XLA Modules:
  0.0 59.9 jit_solution(4400024007037084106)
XLA Ops:
  0.0 58.9 %relation_grads.1 = bf16[8,16,4096]{2,1,0:T(8,128)(2,1)S(1)} custom-call(bf16[8,512,256]{2,1,0:T(8,128)(2,1)} %bitcast.4, bf16[8,16,4096]{2,1,0:T(8,128)(2,1)} %bitcast.5), custom_call_target="tpu_custom_call" | custom-call | tf_op jit(solution)/shard_map/relation_grads/pallas_call | solution.py:179
  58.9 1.0 %copy.4 = bf16[1,8,16,4096]{3,2,1,0:T(8,128)(2,1)} copy(bf16[1,8,16,4096]{3,2,1,0:T(8,128)(2,1)S(1)} %bitcast.3) | data formatting | bytes 2097152

commit v4 on v3

--- a/solution.py
+++ b/solution.py
@@ -25,9 +25,18 @@
     return weights * (1.0 / jnp.sum(weights, axis=0, keepdims=True))
 
 
-def item_gradient(heads, teacher, student, grads, diff):
+def teacher_side(heads, teacher, known):
     length = teacher.shape[0]
-    tw, sw = teacher.shape[1] // heads, student.shape[1] // heads
+    tw = teacher.shape[1] // heads
+    for head in range(heads):
+        th = teacher[:, head * tw : (head + 1) * tw]
+        for i in range(0, length, STRIP):
+            known[head, :, i : i + STRIP] = probs(th, th[i : i + STRIP], LOG2E / math.sqrt(tw))
+
+
+def item_gradient(heads, known, student, grads, diff):
+    length = student.shape[0]
+    sw = student.shape[1] // heads
     x = student[...]
     lane = lax.broadcasted_iota(jnp.int32, x.shape, 1)
     x_t = x.T
@@ -35,11 +44,9 @@
     for head in range(heads):
         mine = (lane >= head * sw) & (lane < (head + 1) * sw)
         xh = jnp.where(mine, x, jnp.zeros_like(x))
-        th = teacher[:, head * tw : (head + 1) * tw]
         for i in range(0, length, STRIP):
             student_probs = probs(x, xh[i : i + STRIP], LOG2E / math.sqrt(sw))
-            teacher_probs = probs(th, th[i : i + STRIP], LOG2E / math.sqrt(tw))
-            diff[:, i : i + STRIP] = (student_probs - teacher_probs).astype(BF16)
+            diff[:, i : i + STRIP] = (student_probs - known[head, :, i : i + STRIP]).astype(BF16)
         xh_t = x_t[head * sw : (head + 1) * sw]
         d = diff[...]
         key_side = lax.dot_general(xh_t, d, NT, preferred_element_type=F32)
@@ -49,7 +56,7 @@
     grads[...] = grads_t.T.astype(BF16)
 
 
-def kernel(ny, nz, heads, teacher_hbm, student_hbm, out, teacher, xs, grads, diff, sems, in_recv, t_sem, level_sem):
+def kernel(ny, nz, heads, teacher_hbm, student_hbm, out, teacher, xs, grads, known, diff, sems, in_recv, t_sem, level_sem):
     n = ny * nz
     me = lax.axis_index("head")
     y, z = me // nz, me % nz
@@ -128,13 +135,19 @@
             all_chunks(level, level)
     all_chunks(EARLY + 1, farthest)
 
+    def ahead(b, _):
+        pltpu.make_async_copy(teacher_hbm.at[b], teacher.at[b], t_sem.at[b]).wait()
+        teacher_side(heads, teacher.at[b], known.at[b])
+        return 0
+
+    lax.fori_loop(0, items, ahead, 0)
+
     def work(c, _):
         batch = pl.ds(c * CHUNK, CHUNK)
         pltpu.make_async_copy(xs.at[batch], xs.at[batch], in_recv.at[c]).wait()
         for k in range(CHUNK):
             b = c * CHUNK + k
-            pltpu.make_async_copy(teacher_hbm.at[b], teacher.at[b], t_sem.at[b]).wait()
-            item_gradient(heads, teacher.at[b], xs.at[b], grads.at[b], diff)
+            item_gradient(heads, known.at[b], xs.at[b], grads.at[b], diff)
         pltpu.make_async_copy(
             grads.at[batch, my_rows, :], out.at[batch, :, my_cols], out_recv
         ).start()
@@ -185,6 +198,7 @@
                 pltpu.VMEM((items, length, teacher_width), BF16),
                 pltpu.VMEM((items, length, width), BF16),
                 pltpu.VMEM((items, length, width), BF16),
+                pltpu.VMEM((items, heads, length, length), F32),
                 pltpu.VMEM((length, length), BF16),
                 pltpu.SemaphoreType.DMA((3,)),
                 pltpu.SemaphoreType.DMA((items // CHUNK,)),

time: 60 us -> 58.1 us (0.968)
  Pallas kernels: 58.9 us -> 57 us
    pallas_call x1, Pallas kernels: 58.9 us -> 57 us  [body(): pl.pallas_call(functools.partial(kernel, n // nz, nz, heads), out_shape=p...]
where the time goes in v4:
time: 58.1 us; the launch traced here: 58 us
  Pallas kernels  57 us (98%)
  local copies, waits for them, and re-layouts  0.97 us (2%)
    pallas_call x1, Pallas kernels, body(): pl.pallas_call(functools.partial(kernel, n // nz, nz, heads), out_shape=p...  57 us

profile of v4, /device:TPU:6, one launch (start us, length us, event | category | flops | bytes accessed | tf_op | source)
XLA Modules:
  0.0 58.0 jit_solution(7501113145234464762)
XLA Ops:
  0.0 57.0 %relation_grads.1 = bf16[8,16,4096]{2,1,0:T(8,128)(2,1)S(1)} custom-call(bf16[8,512,256]{2,1,0:T(8,128)(2,1)} %bitcast.4, bf16[8,16,4096]{2,1,0:T(8,128)(2,1)} %bitcast.5), custom_call_target="tpu_custom_call" | custom-call | tf_op jit(solution)/shard_map/relation_grads/pallas_call | solution.py:192
  57.0 1.0 %copy.4 = bf16[1,8,16,4096]{3,2,1,0:T(8,128)(2,1)} copy(bf16[1,8,16,4096]{3,2,1,0:T(8,128)(2,1)S(1)} %bitcast.3) | data formatting | bytes 2097152

commit v5 on v4

--- a/solution.py
+++ b/solution.py
@@ -68,8 +68,6 @@
         pltpu.make_async_copy(teacher_hbm.at[b], teacher.at[b], t_sem.at[b]).start()
         return 0
 
-    lax.fori_loop(0, items, load_teacher, 0)
-
     def near(act):
         for step in (1, ny - 1):
             act((y + step) % ny, z)
@@ -113,6 +111,8 @@
     near(lambda yy, zz: pl.semaphore_signal(
         barrier, inc=1, device_id={"head": yy * nz + zz}, device_id_type=MESH
     ))
+
+    lax.fori_loop(0, items, load_teacher, 0)
 
     def own(c, _):
         batch = pl.ds(c * CHUNK, CHUNK)
@@ -167,8 +167,10 @@
 
         @pl.when(c == last)
         def _():
-            for hops in range(farthest, 0, -1):
-                peers(send_out, hops, hops)
+            ways = [(dy, dz) for dy in range(-((ny - 1) // 2), ny // 2 + 1) for dz in range(1 - nz, nz) if dy or dz]
+            for dy, dz in sorted(ways, key=lambda way: 1.5 * way[1] - abs(way[0]) - abs(way[1])):
+                to = lambda dy=dy, dz=dz: send_out((y + dy + ny) % ny * nz + z + dz)
+                pl.when((z + dz >= 0) & (z + dz < nz))(to)
 
         return 0
 

time: 58.1 us -> 57.7 us (level)
  no operation moved by 1% of the time
where the time goes in v5:
time: 57.7 us; the launch traced here: 57.6 us
  Pallas kernels  56.6 us (98%)
  local copies, waits for them, and re-layouts  0.97 us (2%)
    pallas_call x1, Pallas kernels, body(): pl.pallas_call(functools.partial(kernel, n // nz, nz, heads), out_shape=p...  56.6 us

profile of v5, /device:TPU:6, one launch (start us, length us, event | category | flops | bytes accessed | tf_op | source)
XLA Modules:
  0.0 57.6 jit_solution(11949969691934174690)
XLA Ops:
  0.0 56.6 %relation_grads.1 = bf16[8,16,4096]{2,1,0:T(8,128)(2,1)S(1)} custom-call(bf16[8,512,256]{2,1,0:T(8,128)(2,1)} %bitcast.4, bf16[8,16,4096]{2,1,0:T(8,128)(2,1)} %bitcast.5), custom_call_target="tpu_custom_call" | custom-call | tf_op jit(solution)/shard_map/relation_grads/pallas_call | solution.py:194
  56.6 1.0 %copy.4 = bf16[1,8,16,4096]{3,2,1,0:T(8,128)(2,1)} copy(bf16[1,8,16,4096]{3,2,1,0:T(8,128)(2,1)S(1)} %bitcast.3) | data formatting | bytes 2097152
